TPU v7x, 128 devices: a whole 4x4x4 slice. The times are simulated.
128 devices in a mesh: view: 4 (over y), tile: 32 (over z, x, core).
Axes of the slice: x: 4, y: 4, z: 4, core: 2. Of those that a mesh axis runs over, the one named last changes fastest.
Arguments:
- estimate: float32 [128, 768, 512], P(None, 'tile'), may hold values from 0.5 to 2
- view_stacks: float32 [4, 128, 768, 512], P('view', 'tile'), may hold values from 0 to 4
- profile_z: float32 [4, 31], P('view'), may hold values from 0.2 to 1
- profile_y: float32 [4, 15], P('view'), may hold values from 0.2 to 1
- profile_x: float32 [4, 15], P('view'), may hold values from 0.2 to 1
- offsets: int32 [4], P('view'), may hold values from -16 to 16, as said below
- coverage: int32 [32, 4], P('tile'), may hold values from 0 to 1, as said below
Outputs:
- new_estimate: float32 [128, 768, 512], P(None, 'tile')
Inputs may be any that keep to these rules, and one draw needn't show every extreme that they name: `offsets`: some view has offset 16 and some view has offset -16. `coverage`: every tile is intersected by at least one view.
All inputs are finite; a program needn't handle non-finite values.
Results may differ from a plain program's by a relative error of at most 0.0001.
Values sent between devices are 32-bit elements; how exact they have to be, the bound alone decides.
A program may use at most 192 MiB of HBM per device.

v0:
```python
import jax
import jax.numpy as jnp
from jax import lax
from jax.sharding import PartitionSpec as P

MAXOFF = 16


def with_halo(cells, sides, width):
    for axis, dim in sides:
        count = lax.axis_size(axis)
        ends = count - 1
        head = lax.slice_in_dim(cells, 0, width, axis=dim)
        tail = lax.slice_in_dim(cells, cells.shape[dim] - width, cells.shape[dim], axis=dim)
        cells = jnp.concatenate(
            [
                lax.ppermute(tail, axis, [(i, (i + 1) % count) for i in range(ends)]),
                cells,
                lax.ppermute(head, axis, [((i + 1) % count, i) for i in range(ends)]),
            ],
            axis=dim,
        )
    return cells


def band_matrix(kernel, rows_out):
    taps_count = kernel.shape[0]
    rows_in = rows_out + taps_count - 1
    out_index = jnp.arange(rows_out, dtype=jnp.int32)
    in_index = jnp.arange(rows_in, dtype=jnp.int32)
    distance = in_index[None, :] - out_index[:, None]
    tap_index = jnp.arange(taps_count, dtype=jnp.int32)
    hits = (distance[None, :, :] == tap_index[:, None, None]).astype(jnp.float32)
    return jnp.sum(hits * kernel[:, None, None], axis=0)


def band_blur(field, kernel, along):
    highest = lax.Precision.HIGHEST
    taps_count = kernel.shape[0]
    half = (taps_count - 1) // 2
    extent = field.shape[along]
    block = min(128, extent)
    count = extent // block
    widths = [(0, 0), (0, 0), (0, 0)]
    widths[along] = (half, block - half)
    padded = jnp.pad(field, widths)
    band = band_matrix(kernel, block)
    head_band = band[:, :block]
    tail_band = band[:, block:]
    head = lax.slice_in_dim(padded, 0, count * block, axis=along)
    tail = lax.slice_in_dim(padded, block, (count + 1) * block, axis=along)
    if along == 0:
        head = head.reshape((count, block) + field.shape[1:])
        tail = tail.reshape((count, block) + field.shape[1:])[:, : taps_count - 1]
        result = jnp.einsum(
            "jbyx,ob->joyx", head, head_band, precision=highest, preferred_element_type=jnp.float32
        )
        result = result + jnp.einsum(
            "jbyx,ob->joyx", tail, tail_band, precision=highest, preferred_element_type=jnp.float32
        )
        return result.reshape(field.shape)
    head = head.reshape(field.shape[:2] + (count, block))
    tail = tail.reshape(field.shape[:2] + (count, block))[..., : taps_count - 1]
    result = jnp.einsum(
        "zyjb,ob->zyjo", head, head_band, precision=highest, preferred_element_type=jnp.float32
    )
    result = result + jnp.einsum(
        "zyjb,ob->zyjo", tail, tail_band, precision=highest, preferred_element_type=jnp.float32
    )
    return result.reshape(field.shape)


def blur_rows(field, matrix_y, weights_z, weights_x):
    highest = lax.Precision.HIGHEST
    result = band_blur(field, weights_z, 0)
    result = jnp.einsum(
        "ya,zax->zyx", matrix_y, result, precision=highest, preferred_element_type=jnp.float32
    )
    return band_blur(result, weights_x, 2)


def on_device(estimate, view_stacks, profile_z, profile_y, profile_x, offsets, coverage):
    weights_z = profile_z[0] / jnp.sum(profile_z[0])
    weights_y = profile_y[0] / jnp.sum(profile_y[0])
    weights_x = profile_x[0] / jnp.sum(profile_x[0])
    row_count = estimate.shape[1]
    x_cells = estimate.shape[2]
    half_y = (weights_y.shape[0] - 1) // 2
    padded = jnp.pad(view_stacks[0], ((0, 0), (0, 0), (MAXOFF, MAXOFF)))
    shifted = lax.dynamic_slice_in_dim(padded, MAXOFF + offsets[0], x_cells, 2)
    stacked = lax.all_to_all(shifted, "tile", split_axis=1, concat_axis=0, tiled=True)
    flipped = weights_y[::-1]
    back_z = weights_z[::-1]
    back_x = weights_x[::-1]
    estimate_ext = with_halo(estimate, (("tile", 1),), half_y)
    blurred = blur_rows(estimate_ext, band_matrix(weights_y, row_count), weights_z, weights_x)
    quotient = stacked / blurred
    quotient_ext = with_halo(quotient, (("tile", 1),), half_y)
    back_blur = blur_rows(quotient_ext, band_matrix(flipped, row_count), back_z, back_x)
    view_index = lax.axis_index("view")
    covered = lax.dynamic_index_in_dim(coverage[0], view_index, 0, keepdims=False).astype(
        jnp.float32
    )
    view_count = jnp.sum(coverage[0]).astype(jnp.float32)
    weighted = covered * back_blur
    summed = lax.psum(weighted, "view")
    return estimate * summed / view_count


def solution(mesh):
    return jax.shard_map(
        on_device,
        mesh=mesh,
        in_specs=(
            P(None, "tile", None),
            P("view", "tile", None, None),
            P("view", None),
            P("view", None),
            P("view", None),
            P("view"),
            P("tile", None),
        ),
        out_specs=P(None, "tile", None),
        check_vma=False,
    )
```

profile of v0, /device:TPU:1, one launch (start us, length us, event | category | flops | bytes accessed | tf_op | source)
XLA Modules:
  0.0 461.1 jit_solution(2243969198912554570)
XLA Ops:
  6.5 6.4 %copy.65 = f32[128,24,512]{2,0,1:T(8,128)S(1)} copy(f32[128,24,512]{2,1,0:T(8,128)} %param.7) | data formatting | bytes 12582912 | tf_op args[0]
  13.0 2.7 copy-done
  15.7 2.2 fusion.39
  17.9 4.7 %collective-permute-start = (f32[128,7,512]{2,0,1:T(8,128)}, f32[128,7,512]{2,0,1:T(8,128)S(1)}, u32[]{:S(2)}, u32[]{:S(2)}) collective-permute-start(f32[128,7,512]{2,0,1:T(8,128)} %get-tuple-element.17), channel_id=1, source_target_pairs={{0,1},{1,2},{2,3},{3,4},{4,5},{5,6},{6,7},{7,8},{8,9},{9,10},{10,1... | collective-permute-start | bytes 5505032 | tf_op jit(solution)/shard_map/ppermute | solution.py:17
  22.7 2.1 collective-permute-start.1
  25.4 6.7 %copy.107 = f32[1,4,768,512]{3,1,2,0:T(4,128)} copy(f32[1,4,768,512]{3,2,1,0:T(8,128)S(1)} %copy-done.4) | data formatting | bytes 12582912 | tf_op args[1]
  32.1 8.7 %pad_dynamic-slice_fusion = f32[4,768,512]{2,0,1:T(4,128)} fusion(s32[]{:T(128)S(6)} %select_n.8, f32[4,768,512]{2,0,1:T(4,128)} %bitcast.76), kind=kLoop, calls=%fused_computation.21 | loop fusion | bytes 12582916 | tf_op jit(solution)/shard_map/dynamic_slice | solution.py:90
  40.9 8.7 %all-to-all-start = ((f32[4,768,512]{2,0,1:T(4,128)}), f32[4,768,512]{2,0,1:T(4,128)}, u32[]{:S(2)}, u32[]{:S(2)}) async-start(f32[4,768,512]{2,0,1:T(4,128)} %pad_dynamic-slice_fusion), calls=%async_computation | async-start | bytes 12582912 | tf_op jit(solution)/shard_map/all_to_all | solution.py:91
  50.1 0.6 reduce_sum.90
  50.8 0.6 reduce_sum.93
  51.5 0.6 reduce_sum.95
  52.2 0.6 broadcast_divide_fusion.2
  53.8 0.6 broadcast_divide_fusion.4
  55.0 11.0 %select_maximum_fusion.2 = f32[256,38,512]{2,0,1:T(8,128)} fusion(f32[128,7,512]{2,0,1:T(8,128)} %collective-permute-done.1, f32[128,24,512]{2,0,1:T(8,128)} %copy-done, f32[128,7,512]{2,0,1:T(8,128)S(1)} %collective-permute-done), kind=kLoop, calls=%fused_computation.4 | loop fusion | flops 39845888 | bytes 29884416 | tf_op jit(solution)/shard_map/concatenate | solution.py:15
  66.0 9.5 %slice_bitcast_fusion.1 = f32[1,128,38,512]{3,1,2,0:T(8,128)} fusion(f32[256,38,512]{2,0,1:T(8,128)} %select_maximum_fusion.2), kind=kLoop, calls=%fused_computation.14 | loop fusion | bytes 19922944 | tf_op jit(solution)/shard_map/reshape | solution.py:54
  75.5 9.8 %fusion.31 = f32[128,38,512]{2,0,1:T(8,128)S(1)} fusion(f32[1,128,38,512]{3,1,2,0:T(8,128)} %slice_bitcast_fusion.1, f32[128,158]{0,1:T(8,128)S(1)} %get-tuple-element.6), kind=kOutput, calls=%fused_computation.41 | convolution fusion | flops 896532480 | bytes 12468224 | tf_op jit(solution)/shard_map/jbyx,ob->joyx/dot_general | solution.py:58
  85.3 15.1 %fusion.13 = f32[128,38,512]{2,0,1:T(8,128)S(1)} fusion(f32[128,38,512]{2,0,1:T(8,128)S(1)} %fusion.31, f32[256,38,512]{2,0,1:T(8,128)} %select_maximum_fusion.2, f32[128,158]{0,1:T(8,128)S(1)} %get-tuple-element.6), kind=kOutput, calls=%fused_computation.30 | convolution fusion | flops 3827695616 | bytes 29949952 | tf_op jit(solution)/shard_map/jbyx,ob->joyx/dot_general | solution.py:55
  100.4 18.2 %fusion.24 = f32[128,24,512]{2,1,0:T(8,128)S(1)} fusion(f32[128,38,512]{2,0,1:T(8,128)S(1)} %fusion.13, f32[24,38]{1,0:T(8,128)S(1)} %get-tuple-element.10), kind=kOutput, calls=%fused_computation.33 | convolution fusion | flops 717225984 | bytes 16256576 | tf_op jit(solution)/shard_map/ya,zax->zyx/dot_general | solution.py:76
  118.6 6.4 %pad_slice_fusion.3 = (f32[128,24,512]{2,1,0:T(8,128)}, f32[128,24,512]{2,1,0:T(8,128)}) fusion(f32[128,24,512]{2,1,0:T(8,128)S(1)} %fusion.24), kind=kLoop, calls=%fused_computation.20 | loop fusion | bytes 18874368 | tf_op jit(solution)/shard_map/slice | solution.py:50
  125.0 6.6 %copy.83 = f32[128,24,512]{0,2,1:T(8,128)} copy(f32[128,24,512]{2,1,0:T(8,128)} %get-tuple-element.16) | data formatting | bytes 12582912 | tf_op jit(solution)/shard_map/reshape | solution.py:63
  131.6 7.6 %reshape.113 = f32[128,24,4,128]{3,2,1,0:T(4,128)} reshape(f32[128,24,512]{2,1,0:T(8,128)} %get-tuple-element.15) | data formatting | bytes 12582912 | tf_op jit(solution)/shard_map/reshape | solution.py:62
  139.1 6.5 %fusion.34 = f32[128,24,4,128]{0,3,2,1:T(8,128)S(1)} fusion(f32[128,24,4,128]{0,3,2,1:T(8,128)} %bitcast.84, f32[128,142]{0,1:T(8,128)S(1)} %get-tuple-element.8), kind=kOutput, calls=%fused_computation.47 | convolution fusion | flops 264241152 | bytes 7086080 | tf_op jit(solution)/shard_map/zyjb,ob->zyjo/dot_general | solution.py:67
  145.6 10.5 %fusion.19 = f32[128,24,4,128]{0,3,2,1:T(8,128)} fusion(f32[128,24,4,128]{0,3,2,1:T(8,128)S(1)} %fusion.34, f32[128,24,4,128]{3,2,1,0:T(4,128)S(1)} %copy-done.3, f32[128,142]{0,1:T(8,128)S(1)} %get-tuple-element.8), kind=kOutput, calls=%fused_computation.32 | convolution fusion | flops 2417491968 | bytes 18939904 | tf_op jit(solution)/shard_map/zyjb,ob->zyjo/dot_general | solution.py:64
  156.1 6.6 %copy.73 = f32[128,24,512]{2,0,1:T(8,128)} copy(f32[128,24,512]{0,2,1:T(8,128)} %bitcast.81) | data formatting | bytes 12582912 | tf_op jit(solution)/shard_map/reshape | solution.py:70
  162.7 5.0 %copy.62 = f32[4,768,512]{2,1,0:T(8,128)S(1)} copy(f32[4,768,512]{2,0,1:T(4,128)} %all-to-all-done) | data formatting | bytes 12582912 | tf_op jit(solution)/shard_map/all_to_all | solution.py:91
  167.6 1.0 copy.63
  169.2 4.2 copy_divide_fusion
  173.5 2.7 copy-done.1
  176.2 2.2 fusion.38
  178.3 3.5 collective-permute-start.2
  181.9 1.9 collective-permute-start.3
  183.8 0.6 fusion.40
  184.4 17.9 %collective-permute-done.2 = f32[128,7,512]{2,0,1:T(8,128)S(1)} collective-permute-done((f32[128,7,512]{2,0,1:T(8,128)}, f32[128,7,512]{2,0,1:T(8,128)S(1)}, u32[]{:S(2)}, u32[]{:S(2)}) %collective-permute-start.2) | collective-permute-done | bytes 1835040 | tf_op jit(solution)/shard_map/ppermute | solution.py:17
  202.3 4.4 collective-permute-done.3
  206.7 11.2 %select_maximum_fusion = f32[256,38,512]{2,0,1:T(8,128)} fusion(f32[128,7,512]{2,0,1:T(8,128)} %collective-permute-done.3, f32[128,24,512]{2,0,1:T(8,128)} %copy-done.1, f32[128,7,512]{2,0,1:T(8,128)S(1)} %collective-permute-done.2), kind=kLoop, calls=%fused_computation.2 | loop fusion | flops 39845888 | bytes 29884416 | tf_op jit(solution)/shard_map/concatenate | solution.py:15
  217.9 9.5 %slice_bitcast_fusion = f32[1,128,38,512]{3,1,2,0:T(8,128)} fusion(f32[256,38,512]{2,0,1:T(8,128)} %select_maximum_fusion), kind=kLoop, calls=%fused_computation.11 | loop fusion | bytes 19922944 | tf_op jit(solution)/shard_map/reshape | solution.py:54
  227.5 9.8 %fusion.30 = f32[128,38,512]{2,0,1:T(8,128)S(1)} fusion(f32[1,128,38,512]{3,1,2,0:T(8,128)} %slice_bitcast_fusion, f32[128,158]{0,1:T(8,128)S(1)} %get-tuple-element.5), kind=kOutput, calls=%fused_computation.39 | convolution fusion | flops 896532480 | bytes 12468224 | tf_op jit(solution)/shard_map/jbyx,ob->joyx/dot_general | solution.py:58
  237.2 15.5 %fusion.16 = f32[128,38,512]{2,0,1:T(8,128)S(1)} fusion(f32[128,38,512]{2,0,1:T(8,128)S(1)} %fusion.30, f32[256,38,512]{2,0,1:T(8,128)} %select_maximum_fusion, f32[128,158]{0,1:T(8,128)S(1)} %get-tuple-element.5), kind=kOutput, calls=%fused_computation.31 | convolution fusion | flops 3827695616 | bytes 29949952 | tf_op jit(solution)/shard_map/jbyx,ob->joyx/dot_general | solution.py:55
  252.7 18.0 %fusion.27 = f32[128,24,512]{2,1,0:T(8,128)S(1)} fusion(f32[128,38,512]{2,0,1:T(8,128)S(1)} %fusion.16, f32[24,38]{1,0:T(8,128)S(1)} %get-tuple-element.9), kind=kOutput, calls=%fused_computation.34 | convolution fusion | flops 717225984 | bytes 16256576 | tf_op jit(solution)/shard_map/ya,zax->zyx/dot_general | solution.py:76
  270.8 6.4 %pad_slice_fusion.1 = (f32[128,24,512]{2,1,0:T(8,128)}, f32[128,24,512]{2,1,0:T(8,128)}) fusion(f32[128,24,512]{2,1,0:T(8,128)S(1)} %fusion.27), kind=kLoop, calls=%fused_computation.18 | loop fusion | bytes 18874368 | tf_op jit(solution)/shard_map/slice | solution.py:50
  277.2 6.6 %copy.84 = f32[128,24,512]{0,2,1:T(8,128)} copy(f32[128,24,512]{2,1,0:T(8,128)} %get-tuple-element.12) | data formatting | bytes 12582912 | tf_op jit(solution)/shard_map/reshape | solution.py:63
  283.7 7.6 %reshape.118 = f32[128,24,4,128]{3,2,1,0:T(4,128)} reshape(f32[128,24,512]{2,1,0:T(8,128)} %get-tuple-element.11) | data formatting | bytes 12582912 | tf_op jit(solution)/shard_map/reshape | solution.py:62
  291.3 6.5 %fusion.32 = f32[128,24,4,128]{0,3,2,1:T(8,128)S(1)} fusion(f32[128,24,4,128]{0,3,2,1:T(8,128)} %bitcast.83, f32[128,142]{0,1:T(8,128)S(1)} %get-tuple-element.7), kind=kOutput, calls=%fused_computation.45 | convolution fusion | flops 264241152 | bytes 7086080 | tf_op jit(solution)/shard_map/zyjb,ob->zyjo/dot_general | solution.py:67
  297.8 11.4 %add_multiply_fusion = f32[128,24,4,128]{0,3,2,1:T(8,128)} fusion(f32[128,24,4,128]{0,3,2,1:T(8,128)S(1)} %fusion.32, f32[]{:T(128)} %bitcast, f32[128,24,4,128]{3,2,1,0:T(4,128)S(1)} %copy-done.2, f32[128,142]{0,1:T(8,128)S(1)} %get-tuple-element.7), kind=kOutput, calls=%fused_computation.29 | convolution fusion | flops 2419064832 | bytes 18939908 | tf_op jit(solution)/shard_map/zyjb,ob->zyjo/dot_general | solution.py:64
  309.2 6.7 %copy.78 = f32[128,24,512]{2,1,0:T(8,128)} copy(f32[128,24,512]{0,2,1:T(8,128)} %bitcast.80) | data formatting | bytes 12582912 | tf_op jit(solution)/shard_map/mul | solution.py:105
  315.9 0.6 reduce_sum.99
  317.2 127.9 %all-reduce.7.cloned.1.call-done = f32[128,24,512]{2,1,0:T(8,128)} async-done(((f32[128,24,512]{2,1,0:T(8,128)}), f32[128,24,512]{2,1,0:T(8,128)}) %all-reduce.7.cloned.1.call-update) | async-done | bytes 6291472 | tf_op jit(solution)/shard_map/psum | solution.py:106
  445.1 8.9 %multiply_divide_fusion = f32[128,24,512]{2,1,0:T(8,128)} fusion(f32[128,24,512]{2,1,0:T(8,128)} %param.7, f32[128,24,512]{2,1,0:T(8,128)} %all-reduce.7.cloned.1.call-done, f32[]{:T(128)S(6)} %convert_element_type.25), kind=kLoop, calls=%fused_computation.28 | loop fusion | flops 3145728 | bytes 18874372 | tf_op jit(solution)/shard_map/div | solution.py:107
  (36 shorter events, 2.9 us)
Async XLA Ops:
  13.0 2.7 copy-start
  15.7 9.8 %copy-start.4 = (f32[1,4,768,512]{3,2,1,0:T(8,128)S(1)}, f32[1,4,768,512]{3,2,1,0:T(8,128)}, u32[]{:S(2)}) copy-start(f32[1,4,768,512]{3,2,1,0:T(8,128)} %param.8) | copy-start | bytes 18874372
  17.9 37.0 %collective-permute-start = (f32[128,7,512]{2,0,1:T(8,128)}, f32[128,7,512]{2,0,1:T(8,128)S(1)}, u32[]{:S(2)}, u32[]{:S(2)}) collective-permute-start(f32[128,7,512]{2,0,1:T(8,128)} %get-tuple-element.17), channel_id=1, source_target_pairs={{0,1},{1,2},{2,3},{3,4},{4,5},{5,6},{6,7},{7,8},{8,9},{9,10},{10,1... | collective-permute-start | bytes 5505032 | tf_op jit(solution)/shard_map/ppermute | solution.py:17
  22.7 32.3 %collective-permute-start.1 = (f32[128,7,512]{2,0,1:T(8,128)}, f32[128,7,512]{2,0,1:T(8,128)}, u32[]{:S(2)}, u32[]{:S(2)}) collective-permute-start(f32[128,7,512]{2,0,1:T(8,128)} %get-tuple-element.18), channel_id=1, source_target_pairs={{1,0},{2,1},{3,2},{4,3},{5,4},{6,5},{7,6},{8,7},{9,8},{10,9},{11,1... | collective-permute-start | bytes 5505032 | tf_op jit(solution)/shard_map/ppermute | solution.py:19
  40.9 9.2 %copy-start.7 = (f32[1,31]{1,0:T(1,128)S(1)}, f32[1,31]{1,0:T(1,128)}, u32[]{:S(2)}) copy-start(f32[1,31]{1,0:T(1,128)} %param.9) | copy-start | bytes 376
  40.9 9.9 %copy-start.5 = (f32[1,15]{1,0:T(1,128)S(1)}, f32[1,15]{1,0:T(1,128)}, u32[]{:S(2)}) copy-start(f32[1,15]{1,0:T(1,128)} %param.10) | copy-start | bytes 184
  40.9 10.6 %copy-start.6 = (f32[1,15]{1,0:T(1,128)S(1)}, f32[1,15]{1,0:T(1,128)}, u32[]{:S(2)}) copy-start(f32[1,15]{1,0:T(1,128)} %param.11) | copy-start | bytes 184
  40.9 121.8 %all-to-all-start = ((f32[4,768,512]{2,0,1:T(4,128)}), f32[4,768,512]{2,0,1:T(4,128)}, u32[]{:S(2)}, u32[]{:S(2)}) async-start(f32[4,768,512]{2,0,1:T(4,128)} %pad_dynamic-slice_fusion), calls=%async_computation | async-start | bytes 12582912 | tf_op jit(solution)/shard_map/all_to_all | solution.py:91
  49.6 395.5 %all-reduce.7.cloned.1.call-start = ((), (), s32[]{:S(2)}) async-start(), calls=%async_computation.1 | async-start | bytes 12582912 | tf_op jit(solution)/shard_map/psum | solution.py:106
  139.1 6.5 %copy-start.3 = (f32[128,24,4,128]{3,2,1,0:T(4,128)S(1)}, f32[128,24,4,128]{3,2,1,0:T(4,128)}, u32[]{:S(2)}) copy-start(f32[128,24,4,128]{3,2,1,0:T(4,128)} %reshape.113) | copy-start | bytes 18874372
  162.7 6.0 %slice-start = ((s8[6291456]{0:T(1024)(128)(4,1)}), s8[4194304]{0:T(1024)(128)(4,1)S(1)}, s32[]{:S(2)}) async-start(s8[6291456]{0:T(1024)(128)(4,1)} %bitcast.78), calls=%async_computation.2 | async-start | bytes 8388608
  167.6 1.6 slice-start.1
  173.5 2.7 copy-start.1
  176.2 7.6 %copy-start.8 = (s32[1,4]{1,0:T(1,128)S(1)}, s32[1,4]{1,0:T(1,128)}, u32[]{:S(2)}) copy-start(s32[1,4]{1,0:T(1,128)} %param.13) | copy-start | bytes 52
  178.3 24.0 %collective-permute-start.2 = (f32[128,7,512]{2,0,1:T(8,128)}, f32[128,7,512]{2,0,1:T(8,128)S(1)}, u32[]{:S(2)}, u32[]{:S(2)}) collective-permute-start(f32[128,7,512]{2,0,1:T(8,128)} %get-tuple-element.13), channel_id=1, source_target_pairs={{0,1},{1,2},{2,3},{3,4},{4,5},{5,6},{6,7},{7,8},{8,9},{9,10},{10,1... | collective-permute-start | bytes 5505032 | tf_op jit(solution)/shard_map/ppermute | solution.py:17
  181.9 24.9 %collective-permute-start.3 = (f32[128,7,512]{2,0,1:T(8,128)}, f32[128,7,512]{2,0,1:T(8,128)}, u32[]{:S(2)}, u32[]{:S(2)}) collective-permute-start(f32[128,7,512]{2,0,1:T(8,128)} %get-tuple-element.14), channel_id=1, source_target_pairs={{1,0},{2,1},{3,2},{4,3},{5,4},{6,5},{7,6},{8,7},{9,8},{10,9},{11,1... | collective-permute-start | bytes 5505032 | tf_op jit(solution)/shard_map/ppermute | solution.py:19
  291.3 6.5 %copy-start.2 = (f32[128,24,4,128]{3,2,1,0:T(4,128)S(1)}, f32[128,24,4,128]{3,2,1,0:T(4,128)}, u32[]{:S(2)}) copy-start(f32[128,24,4,128]{3,2,1,0:T(4,128)} %reshape.118) | copy-start | bytes 18874372
Sparse Core Ops, SparseCore 0:
  316.0 129.0 all-reduce.6
where the time goes:
time: 466 us; the launch traced here: 461 us
  waiting for transfers between devices  150 us (32%)
  matrix products  121 us (26%)
  local copies, waits for them, and re-layouts  112 us (24%)
  other arithmetic  41 us (9%)
  starting transfers between devices  21.5 us (5%)
  between operations  15.2 us (3%)
    psum x1, waiting for transfers between devices, on_device(): summed = lax.psum(weighted, 'view')  128 us
    dot_general x2, matrix products, blur_rows(): jnp.einsum('ya,zax->zyx', matrix_y, result, precision=highest, preferred_...  36.2 us
    dot_general x2, matrix products, band_blur(): jnp.einsum('jbyx,ob->joyx', head, head_band, precision=highest, preferred...  30.6 us
    concatenate x2, other arithmetic, with_halo(): jnp.concatenate([lax.ppermute(tail, axis, [(i, (i + 1) % count) for i in...  22.2 us
    dot_general x2, matrix products, band_blur(): jnp.einsum('zyjb,ob->zyjo', head, head_band, precision=highest, preferred...  21.9 us
    dot_general x2, matrix products, band_blur(): jnp.einsum('jbyx,ob->joyx', tail, tail_band, precision=highest, preferred...  19.5 us
    reshape x2, local copies, waits for them, and re-layouts, band_blur(): tail = tail.reshape((count, block) + field.shape[1:])[:, :taps_count - 1]  19.1 us
    unnamed x24, local copies, waits for them, and re-layouts  19.1 us
  transfers between devices with their start and end apart: 6, of which 3 were waited for; matrix products, arithmetic and copies ran while one was open for 28% of the time, Pallas kernels for 0%

commit v1 on v0

--- a/solution.py
+++ b/solution.py
@@ -103,7 +103,10 @@
     )
     view_count = jnp.sum(coverage[0]).astype(jnp.float32)
     weighted = covered * back_blur
-    summed = lax.psum(weighted, "view")
+    n_dev, summed = (lax.axis_size("view"), weighted)
+    for far in [1 << k for k in range(n_dev.bit_length() - 1)]:
+        route = [(i_2, i_2 ^ far) for i_2 in range(n_dev)]
+        summed = summed + lax.ppermute(summed, "view", route)
     return estimate * summed / view_count
 
 

time: 466 us -> 608 us (1.30)
  the two profiles are of different devices: /device:TPU:1 before, /device:TPU:18 now
where the time goes in v1:
time: 608 us; the launch traced here: 604 us
  waiting for transfers between devices  295 us (49%)
  matrix products  121 us (20%)
  local copies, waits for them, and re-layouts  112 us (18%)
  other arithmetic  50.9 us (8%)
  starting transfers between devices  22.5 us (4%)
    ppermute x2, waiting for transfers between devices, on_device(): summed = summed + lax.ppermute(summed, 'view', route)  275 us
    dot_general x2, matrix products, blur_rows(): jnp.einsum('ya,zax->zyx', matrix_y, result, precision=highest, preferred_...  36.2 us
    dot_general x2, matrix products, band_blur(): jnp.einsum('jbyx,ob->joyx', head, head_band, precision=highest, preferred...  30.6 us
    concatenate x2, other arithmetic, with_halo(): jnp.concatenate([lax.ppermute(tail, axis, [(i, (i + 1) % count) for i in...  22.2 us
    dot_general x2, matrix products, band_blur(): jnp.einsum('zyjb,ob->zyjo', head, head_band, precision=highest, preferred...  21.9 us
    dot_general x2, matrix products, band_blur(): jnp.einsum('jbyx,ob->joyx', tail, tail_band, precision=highest, preferred...  19.5 us
    reshape x2, local copies, waits for them, and re-layouts, band_blur(): tail = tail.reshape((count, block) + field.shape[1:])[:, :taps_count - 1]  19.1 us
    unnamed x24, local copies, waits for them, and re-layouts  19.1 us
  transfers between devices with their start and end apart: 7, of which 4 were waited for; matrix products, arithmetic and copies ran while one was open for 21% of the time, Pallas kernels for 0%

profile of v1, /device:TPU:18, one launch (start us, length us, event | category | flops | bytes accessed | tf_op | source)
XLA Modules:
  0.0 603.5 jit_solution(15853297944864886067)
XLA Ops:
  0.0 6.4 %copy.69 = f32[128,24,512]{2,0,1:T(8,128)S(1)} copy(f32[128,24,512]{2,1,0:T(8,128)} %param.7) | data formatting | bytes 12582912 | tf_op args[0]
  6.4 2.7 copy-done
  9.1 2.2 fusion.39
  11.4 2.2 collective-permute-start
  13.6 3.9 collective-permute-start.1
  18.1 6.7 %copy.112 = f32[1,4,768,512]{3,1,2,0:T(4,128)} copy(f32[1,4,768,512]{3,2,1,0:T(8,128)S(1)} %copy-done.4) | data formatting | bytes 12582912 | tf_op args[1]
  24.8 8.7 %pad_dynamic-slice_fusion = f32[4,768,512]{2,0,1:T(4,128)} fusion(s32[]{:T(128)S(6)} %select_n.8, f32[4,768,512]{2,0,1:T(4,128)} %bitcast.76), kind=kLoop, calls=%fused_computation.21 | loop fusion | bytes 12582916 | tf_op jit(solution)/shard_map/dynamic_slice | solution.py:90
  33.5 9.3 %all-to-all-start = ((f32[4,768,512]{2,0,1:T(4,128)}), f32[4,768,512]{2,0,1:T(4,128)}, u32[]{:S(2)}, u32[]{:S(2)}) async-start(f32[4,768,512]{2,0,1:T(4,128)} %pad_dynamic-slice_fusion), calls=%async_computation | async-start | bytes 12582912 | tf_op jit(solution)/shard_map/all_to_all | solution.py:91
  44.2 0.7 reduce_sum.95
  45.7 0.6 broadcast_divide_fusion
  47.8 11.0 %select_maximum_fusion.2 = f32[256,38,512]{2,0,1:T(8,128)} fusion(f32[128,7,512]{2,0,1:T(8,128)} %collective-permute-done.1, f32[128,24,512]{2,0,1:T(8,128)} %copy-done, f32[128,7,512]{2,0,1:T(8,128)S(1)} %collective-permute-done), kind=kLoop, calls=%fused_computation.4 | loop fusion | flops 39845888 | bytes 29884416 | tf_op jit(solution)/shard_map/concatenate | solution.py:15
  58.8 9.6 %slice_bitcast_fusion.1 = f32[1,128,38,512]{3,1,2,0:T(8,128)} fusion(f32[256,38,512]{2,0,1:T(8,128)} %select_maximum_fusion.2), kind=kLoop, calls=%fused_computation.14 | loop fusion | bytes 19922944 | tf_op jit(solution)/shard_map/reshape | solution.py:54
  68.3 9.8 %fusion.31 = f32[128,38,512]{2,0,1:T(8,128)S(1)} fusion(f32[1,128,38,512]{3,1,2,0:T(8,128)} %slice_bitcast_fusion.1, f32[128,158]{0,1:T(8,128)S(1)} %get-tuple-element.6), kind=kOutput, calls=%fused_computation.41 | convolution fusion | flops 896532480 | bytes 12468224 | tf_op jit(solution)/shard_map/jbyx,ob->joyx/dot_general | solution.py:58
  78.1 15.1 %fusion.13 = f32[128,38,512]{2,0,1:T(8,128)S(1)} fusion(f32[128,38,512]{2,0,1:T(8,128)S(1)} %fusion.31, f32[256,38,512]{2,0,1:T(8,128)} %select_maximum_fusion.2, f32[128,158]{0,1:T(8,128)S(1)} %get-tuple-element.6), kind=kOutput, calls=%fused_computation.30 | convolution fusion | flops 3827695616 | bytes 29949952 | tf_op jit(solution)/shard_map/jbyx,ob->joyx/dot_general | solution.py:55
  93.2 18.2 %fusion.24 = f32[128,24,512]{2,1,0:T(8,128)S(1)} fusion(f32[128,38,512]{2,0,1:T(8,128)S(1)} %fusion.13, f32[24,38]{1,0:T(8,128)S(1)} %get-tuple-element.10), kind=kOutput, calls=%fused_computation.33 | convolution fusion | flops 717225984 | bytes 16256576 | tf_op jit(solution)/shard_map/ya,zax->zyx/dot_general | solution.py:76
  111.4 6.4 %pad_slice_fusion.3 = (f32[128,24,512]{2,1,0:T(8,128)}, f32[128,24,512]{2,1,0:T(8,128)}) fusion(f32[128,24,512]{2,1,0:T(8,128)S(1)} %fusion.24), kind=kLoop, calls=%fused_computation.20 | loop fusion | bytes 18874368 | tf_op jit(solution)/shard_map/slice | solution.py:50
  117.8 6.5 %copy.88 = f32[128,24,512]{0,2,1:T(8,128)} copy(f32[128,24,512]{2,1,0:T(8,128)} %get-tuple-element.16) | data formatting | bytes 12582912 | tf_op jit(solution)/shard_map/reshape | solution.py:63
  124.3 7.6 %reshape.113 = f32[128,24,4,128]{3,2,1,0:T(4,128)} reshape(f32[128,24,512]{2,1,0:T(8,128)} %get-tuple-element.15) | data formatting | bytes 12582912 | tf_op jit(solution)/shard_map/reshape | solution.py:62
  131.9 6.5 %fusion.34 = f32[128,24,4,128]{0,3,2,1:T(8,128)S(1)} fusion(f32[128,24,4,128]{0,3,2,1:T(8,128)} %bitcast.84, f32[128,142]{0,1:T(8,128)S(1)} %get-tuple-element.8), kind=kOutput, calls=%fused_computation.47 | convolution fusion | flops 264241152 | bytes 7086080 | tf_op jit(solution)/shard_map/zyjb,ob->zyjo/dot_general | solution.py:67
  138.4 10.5 %fusion.19 = f32[128,24,4,128]{0,3,2,1:T(8,128)} fusion(f32[128,24,4,128]{0,3,2,1:T(8,128)S(1)} %fusion.34, f32[128,24,4,128]{3,2,1,0:T(4,128)S(1)} %copy-done.3, f32[128,142]{0,1:T(8,128)S(1)} %get-tuple-element.8), kind=kOutput, calls=%fused_computation.32 | convolution fusion | flops 2417491968 | bytes 18939904 | tf_op jit(solution)/shard_map/zyjb,ob->zyjo/dot_general | solution.py:64
  148.9 6.6 %copy.77 = f32[128,24,512]{2,0,1:T(8,128)} copy(f32[128,24,512]{0,2,1:T(8,128)} %bitcast.81) | data formatting | bytes 12582912 | tf_op jit(solution)/shard_map/reshape | solution.py:70
  155.4 5.0 copy.66
  160.4 1.0 copy.67
  162.0 4.2 copy_divide_fusion
  166.3 2.7 copy-done.1
  168.9 2.2 fusion.38
  171.1 2.0 collective-permute-start.2
  173.1 3.5 collective-permute-start.3
  176.7 0.6 fusion.40
  177.3 18.5 %collective-permute-done.2 = f32[128,7,512]{2,0,1:T(8,128)S(1)} collective-permute-done((f32[128,7,512]{2,0,1:T(8,128)}, f32[128,7,512]{2,0,1:T(8,128)S(1)}, u32[]{:S(2)}, u32[]{:S(2)}) %collective-permute-start.2) | collective-permute-done | bytes 1835040 | tf_op jit(solution)/shard_map/ppermute | solution.py:17
  195.8 1.9 collective-permute-done.3
  197.7 11.2 %select_maximum_fusion = f32[256,38,512]{2,0,1:T(8,128)} fusion(f32[128,7,512]{2,0,1:T(8,128)} %collective-permute-done.3, f32[128,24,512]{2,0,1:T(8,128)} %copy-done.1, f32[128,7,512]{2,0,1:T(8,128)S(1)} %collective-permute-done.2), kind=kLoop, calls=%fused_computation.2 | loop fusion | flops 39845888 | bytes 29884416 | tf_op jit(solution)/shard_map/concatenate | solution.py:15
  208.9 9.6 %slice_bitcast_fusion = f32[1,128,38,512]{3,1,2,0:T(8,128)} fusion(f32[256,38,512]{2,0,1:T(8,128)} %select_maximum_fusion), kind=kLoop, calls=%fused_computation.11 | loop fusion | bytes 19922944 | tf_op jit(solution)/shard_map/reshape | solution.py:54
  218.5 9.8 %fusion.30 = f32[128,38,512]{2,0,1:T(8,128)S(1)} fusion(f32[1,128,38,512]{3,1,2,0:T(8,128)} %slice_bitcast_fusion, f32[128,158]{0,1:T(8,128)S(1)} %get-tuple-element.5), kind=kOutput, calls=%fused_computation.39 | convolution fusion | flops 896532480 | bytes 12468224 | tf_op jit(solution)/shard_map/jbyx,ob->joyx/dot_general | solution.py:58
  228.2 15.5 %fusion.16 = f32[128,38,512]{2,0,1:T(8,128)S(1)} fusion(f32[128,38,512]{2,0,1:T(8,128)S(1)} %fusion.30, f32[256,38,512]{2,0,1:T(8,128)} %select_maximum_fusion, f32[128,158]{0,1:T(8,128)S(1)} %get-tuple-element.5), kind=kOutput, calls=%fused_computation.31 | convolution fusion | flops 3827695616 | bytes 29949952 | tf_op jit(solution)/shard_map/jbyx,ob->joyx/dot_general | solution.py:55
  243.7 18.0 %fusion.27 = f32[128,24,512]{2,1,0:T(8,128)S(1)} fusion(f32[128,38,512]{2,0,1:T(8,128)S(1)} %fusion.16, f32[24,38]{1,0:T(8,128)S(1)} %get-tuple-element.9), kind=kOutput, calls=%fused_computation.34 | convolution fusion | flops 717225984 | bytes 16256576 | tf_op jit(solution)/shard_map/ya,zax->zyx/dot_general | solution.py:76
  261.7 6.4 %pad_slice_fusion.1 = (f32[128,24,512]{2,1,0:T(8,128)}, f32[128,24,512]{2,1,0:T(8,128)}) fusion(f32[128,24,512]{2,1,0:T(8,128)S(1)} %fusion.27), kind=kLoop, calls=%fused_computation.18 | loop fusion | bytes 18874368 | tf_op jit(solution)/shard_map/slice | solution.py:50
  268.2 6.5 %copy.89 = f32[128,24,512]{0,2,1:T(8,128)} copy(f32[128,24,512]{2,1,0:T(8,128)} %get-tuple-element.12) | data formatting | bytes 12582912 | tf_op jit(solution)/shard_map/reshape | solution.py:63
  274.7 7.6 %reshape.118 = f32[128,24,4,128]{3,2,1,0:T(4,128)} reshape(f32[128,24,512]{2,1,0:T(8,128)} %get-tuple-element.11) | data formatting | bytes 12582912 | tf_op jit(solution)/shard_map/reshape | solution.py:62
  282.2 6.5 %fusion.32 = f32[128,24,4,128]{0,3,2,1:T(8,128)S(1)} fusion(f32[128,24,4,128]{0,3,2,1:T(8,128)} %bitcast.83, f32[128,142]{0,1:T(8,128)S(1)} %get-tuple-element.7), kind=kOutput, calls=%fused_computation.45 | convolution fusion | flops 264241152 | bytes 7086080 | tf_op jit(solution)/shard_map/zyjb,ob->zyjo/dot_general | solution.py:67
  288.7 11.5 %add_multiply_fusion = f32[128,24,4,128]{0,3,2,1:T(8,128)} fusion(f32[128,24,4,128]{0,3,2,1:T(8,128)S(1)} %fusion.32, f32[]{:T(128)} %bitcast, f32[128,24,4,128]{3,2,1,0:T(4,128)S(1)} %copy-done.2, f32[128,142]{0,1:T(8,128)S(1)} %get-tuple-element.7), kind=kOutput, calls=%fused_computation.29 | convolution fusion | flops 2419064832 | bytes 18939908 | tf_op jit(solution)/shard_map/zyjb,ob->zyjo/dot_general | solution.py:64
  300.2 6.7 %copy.83 = f32[128,24,512]{2,1,0:T(8,128)} copy(f32[128,24,512]{0,2,1:T(8,128)} %bitcast.80) | data formatting | bytes 12582912 | tf_op jit(solution)/shard_map/mul | solution.py:105
  306.9 1.3 collective-permute-start.4
  308.2 136.5 %collective-permute-done.4 = f32[128,24,512]{2,1,0:T(8,128)S(1)} collective-permute-done((f32[128,24,512]{2,1,0:T(8,128)}, f32[128,24,512]{2,1,0:T(8,128)S(1)}, u32[]{:S(2)}, u32[]{:S(2)}) %collective-permute-start.4) | collective-permute-done | bytes 6291488 | tf_op jit(solution)/shard_map/ppermute | solution.py:109
  444.7 7.0 %add.49 = f32[128,24,512]{2,1,0:T(8,128)} add(f32[128,24,512]{2,1,0:T(8,128)} %copy.83, f32[128,24,512]{2,1,0:T(8,128)S(1)} %collective-permute-done.4) | non-fusion elementwise | flops 1572864 | bytes 18874368 | tf_op jit(solution)/shard_map/add | solution.py:109
  452.1 0.7 reduce_sum.99
  453.4 138.2 %collective-permute-done.5 = f32[128,24,512]{2,1,0:T(8,128)} collective-permute-done((f32[128,24,512]{2,1,0:T(8,128)}, f32[128,24,512]{2,1,0:T(8,128)}, u32[]{:S(2)}, u32[]{:S(2)}) %collective-permute-start.5) | collective-permute-done | bytes 6291488 | tf_op jit(solution)/shard_map/ppermute | solution.py:109
  591.6 11.5 %multiply_divide_fusion = f32[128,24,512]{2,1,0:T(8,128)} fusion(f32[128,24,512]{2,1,0:T(8,128)} %param.7, f32[128,24,512]{2,1,0:T(8,128)} %add.49, f32[128,24,512]{2,1,0:T(8,128)} %collective-permute-done.5, f32[]{:T(128)S(6)} %convert_element_type.25), kind=kLoop, calls=%fused_computation.28 | loop fusion | flops 4718592 | bytes 25165828 | tf_op jit(solution)/shard_map/div | solution.py:110
  (38 shorter events, 4.5 us)
Async XLA Ops:
  6.4 2.7 copy-start
  9.1 8.9 %copy-start.4 = (f32[1,4,768,512]{3,2,1,0:T(8,128)S(1)}, f32[1,4,768,512]{3,2,1,0:T(8,128)}, u32[]{:S(2)}) copy-start(f32[1,4,768,512]{3,2,1,0:T(8,128)} %param.8) | copy-start | bytes 18874372
  11.4 36.4 %collective-permute-start = (f32[128,7,512]{2,0,1:T(8,128)}, f32[128,7,512]{2,0,1:T(8,128)S(1)}, u32[]{:S(2)}, u32[]{:S(2)}) collective-permute-start(f32[128,7,512]{2,0,1:T(8,128)} %get-tuple-element.17), channel_id=1, source_target_pairs={{0,1},{1,2},{2,3},{3,4},{4,5},{5,6},{6,7},{7,8},{8,9},{9,10},{10,1... | collective-permute-start | bytes 5505032 | tf_op jit(solution)/shard_map/ppermute | solution.py:17
  13.6 34.2 %collective-permute-start.1 = (f32[128,7,512]{2,0,1:T(8,128)}, f32[128,7,512]{2,0,1:T(8,128)}, u32[]{:S(2)}, u32[]{:S(2)}) collective-permute-start(f32[128,7,512]{2,0,1:T(8,128)} %get-tuple-element.18), channel_id=1, source_target_pairs={{1,0},{2,1},{3,2},{4,3},{5,4},{6,5},{7,6},{8,7},{9,8},{10,9},{11,1... | collective-permute-start | bytes 5505032 | tf_op jit(solution)/shard_map/ppermute | solution.py:19
  33.5 9.3 %copy-start.7 = (f32[1,31]{1,0:T(1,128)S(1)}, f32[1,31]{1,0:T(1,128)}, u32[]{:S(2)}) copy-start(f32[1,31]{1,0:T(1,128)} %param.9) | copy-start | bytes 376
  33.5 10.0 %copy-start.5 = (f32[1,15]{1,0:T(1,128)S(1)}, f32[1,15]{1,0:T(1,128)}, u32[]{:S(2)}) copy-start(f32[1,15]{1,0:T(1,128)} %param.10) | copy-start | bytes 184
  33.5 10.7 %copy-start.6 = (f32[1,15]{1,0:T(1,128)S(1)}, f32[1,15]{1,0:T(1,128)}, u32[]{:S(2)}) copy-start(f32[1,15]{1,0:T(1,128)} %param.11) | copy-start | bytes 184
  33.5 121.9 %all-to-all-start = ((f32[4,768,512]{2,0,1:T(4,128)}), f32[4,768,512]{2,0,1:T(4,128)}, u32[]{:S(2)}, u32[]{:S(2)}) async-start(f32[4,768,512]{2,0,1:T(4,128)} %pad_dynamic-slice_fusion), calls=%async_computation | async-start | bytes 12582912 | tf_op jit(solution)/shard_map/all_to_all | solution.py:91
  131.9 6.5 %copy-start.3 = (f32[128,24,4,128]{3,2,1,0:T(4,128)S(1)}, f32[128,24,4,128]{3,2,1,0:T(4,128)}, u32[]{:S(2)}) copy-start(f32[128,24,4,128]{3,2,1,0:T(4,128)} %reshape.113) | copy-start | bytes 18874372
  155.4 6.0 slice-start
  160.4 1.6 slice-start.1
  166.2 2.7 copy-start.1
  168.9 7.7 %copy-start.8 = (s32[1,4]{1,0:T(1,128)S(1)}, s32[1,4]{1,0:T(1,128)}, u32[]{:S(2)}) copy-start(s32[1,4]{1,0:T(1,128)} %param.13) | copy-start | bytes 52
  171.1 24.7 %collective-permute-start.2 = (f32[128,7,512]{2,0,1:T(8,128)}, f32[128,7,512]{2,0,1:T(8,128)S(1)}, u32[]{:S(2)}, u32[]{:S(2)}) collective-permute-start(f32[128,7,512]{2,0,1:T(8,128)} %get-tuple-element.13), channel_id=1, source_target_pairs={{0,1},{1,2},{2,3},{3,4},{4,5},{5,6},{6,7},{7,8},{8,9},{9,10},{10,1... | collective-permute-start | bytes 5505032 | tf_op jit(solution)/shard_map/ppermute | solution.py:17
  173.1 24.6 %collective-permute-start.3 = (f32[128,7,512]{2,0,1:T(8,128)}, f32[128,7,512]{2,0,1:T(8,128)}, u32[]{:S(2)}, u32[]{:S(2)}) collective-permute-start(f32[128,7,512]{2,0,1:T(8,128)} %get-tuple-element.14), channel_id=1, source_target_pairs={{1,0},{2,1},{3,2},{4,3},{5,4},{6,5},{7,6},{8,7},{9,8},{10,9},{11,1... | collective-permute-start | bytes 5505032 | tf_op jit(solution)/shard_map/ppermute | solution.py:19
  282.2 6.5 %copy-start.2 = (f32[128,24,4,128]{3,2,1,0:T(4,128)S(1)}, f32[128,24,4,128]{3,2,1,0:T(4,128)}, u32[]{:S(2)}) copy-start(f32[128,24,4,128]{3,2,1,0:T(4,128)} %reshape.118) | copy-start | bytes 18874372
  306.9 137.8 %collective-permute-start.4 = (f32[128,24,512]{2,1,0:T(8,128)}, f32[128,24,512]{2,1,0:T(8,128)S(1)}, u32[]{:S(2)}, u32[]{:S(2)}) collective-permute-start(f32[128,24,512]{2,1,0:T(8,128)} %copy.83), channel_id=1, source_target_pairs={{0,32},{32,0},{64,96},{96,64},{1,33},{33,1},{65,97},{97,65},{2,34}... | collective-permute-start | bytes 18874376 | tf_op jit(solution)/shard_map/ppermute | solution.py:109
  451.8 139.8 %collective-permute-start.5 = (f32[128,24,512]{2,1,0:T(8,128)}, f32[128,24,512]{2,1,0:T(8,128)}, u32[]{:S(2)}, u32[]{:S(2)}) collective-permute-start(f32[128,24,512]{2,1,0:T(8,128)} %add.49), channel_id=1, source_target_pairs={{0,64},{32,96},{64,0},{96,32},{1,65},{33,97},{65,1},{97,33},{2,66}... | collective-permute-start | bytes 18874376 | tf_op jit(solution)/shard_map/ppermute | solution.py:109
